TPU v7x, 32 devices: a whole 2x2x4 slice. The times are simulated.
32 devices in a mesh: facet: 8 (over y, x, core), col: 4 (over z).
Axes of the slice: x: 2, y: 2, z: 4, core: 2. Of those that a mesh axis runs over, the one named last changes fastest.
Arguments:
- facets: float32 [2, 8, 24, 2, 4096], P(None, 'facet', None, None, 'col'), may hold values from -6 to 6
- facet_x: int32 [8], P('facet'), may hold values from 0 to 32767
- facet_y: int32 [2], replicated, may hold values from 0 to 32767
- col_u: int32 [8], replicated, may hold values from 0 to 32767
- slot_col: int32 [4, 8], P('col'), may hold values from 0 to 1
- slot_v: int32 [4, 8], P('col'), may hold values from 0 to 32767
Outputs:
- subgrids: float32 [4, 8, 512, 1024], P('col', 'facet')
Inputs may be any that keep to these rules, and one draw needn't show every extreme that they name: `col_u`: offset in the image. `slot_col`: the subgrid's column is owner * 2 + this value. `slot_v`: offset in the image.
All inputs are finite; a program needn't handle non-finite values.
Results may differ from a plain program's by a relative error of at most 0.0003.
Values sent between devices are 32-bit elements; how exact they have to be, the bound alone decides.
A program may use at most 128 MiB of HBM per device.

v0:
```python
import math
import jax
import jax.numpy as jnp
from jax import lax
from jax.sharding import PartitionSpec as P

FS = 4096
SG = 512
COLS_DEV = 2
SLOTS = 1


def mulmod(first_factor, second_factor, modulus):
    upper = first_factor * (second_factor // 512) % modulus
    return (upper * 512 + first_factor * (second_factor % 512)) % modulus


def column_part(real_part, imag_part, shifted, table, col_u, img, count):
    turn = 2.0 * math.pi / img
    column_angle = mulmod(col_u[:, None], shifted[None, :], img).astype(jnp.float32) * turn
    cosine = jnp.cos(column_angle)[:, None, :]
    sine = jnp.sin(column_angle)[:, None, :]
    turned_real = real_part[None] * cosine + imag_part[None] * sine
    turned_imag = imag_part[None] * cosine - real_part[None] * sine
    local_rows = real_part.shape[0]
    width = real_part.shape[1]
    stacked = jnp.stack([turned_real, turned_imag]).reshape(-1, width)
    product = jnp.dot(
        stacked, table, precision=lax.Precision.HIGHEST, preferred_element_type=jnp.float32
    )
    product = product.reshape(2, count, local_rows, 2 * SG)
    from_real = product[0]
    from_imag = product[1]
    real_out = from_real[..., :SG] + from_imag[..., SG:]
    imag_out = from_imag[..., :SG] - from_real[..., SG:]
    return jnp.concatenate([real_out, imag_out], axis=-1)


def slot_term(owned, row_cells, img, column, shift_v):
    turn = 2.0 * math.pi / img
    v_cells = (shift_v + jnp.arange(SG, dtype=jnp.int32)) % img
    angle = mulmod(v_cells[:, None], row_cells[None, :], img).astype(jnp.float32) * turn
    cosine = jnp.cos(angle)
    sine = jnp.sin(angle)
    chosen = lax.dynamic_index_in_dim(owned, column, 0, keepdims=False)
    first = jnp.dot(
        cosine, chosen, precision=lax.Precision.HIGHEST, preferred_element_type=jnp.float32
    )
    second = jnp.dot(
        sine, chosen, precision=lax.Precision.HIGHEST, preferred_element_type=jnp.float32
    )
    real_out = first[:, :SG] + second[:, SG:]
    imag_out = first[:, SG:] - second[:, :SG]
    return jnp.concatenate([real_out, imag_out], axis=-1)


def per_device(facets, facet_x, facet_y, col_u, slot_col, slot_v):
    width = facets.shape[-1]
    band_rows = facets.shape[2]
    img = FS * lax.axis_size("facet")
    turn = 2.0 * math.pi / img
    x_start = lax.axis_index("col") * width
    real_part = facets[:, 0, :, 0, :].reshape(-1, width)
    imag_part = facets[:, 0, :, 1, :].reshape(-1, width)
    shifted = (facet_x[0] + x_start + jnp.arange(width, dtype=jnp.int32)) % img
    u_cells = jnp.arange(SG, dtype=jnp.int32)
    table_angle = mulmod(u_cells[None, :], shifted[:, None], img).astype(jnp.float32) * turn
    table = jnp.concatenate([jnp.cos(table_angle), jnp.sin(table_angle)], axis=1)
    owned = lax.psum_scatter(
        column_part(
            real_part, imag_part, shifted, table, col_u, img, COLS_DEV * lax.axis_size("col")
        ),
        "col",
        scatter_dimension=0,
        tiled=True,
    )
    total_rows = owned.shape[1]
    row_ids = jnp.arange(total_rows, dtype=jnp.int32)
    y_start = jnp.where(row_ids // band_rows == 0, facet_y[0], facet_y[1])
    row_cells = (y_start + row_ids % band_rows) % img
    scale = 1.0 / math.sqrt(2.0 * FS * band_rows * lax.axis_size("facet"))
    owner_cols = slot_col[0]
    owner_shift = slot_v[0]
    merged = lax.psum(owned, "facet")

    def own_slot(slot_id):
        return slot_term(merged, row_cells, img, owner_cols[slot_id], owner_shift[slot_id])

    first_slot = lax.axis_index("facet") * SLOTS
    summed = lax.map(own_slot, first_slot + jnp.arange(SLOTS, dtype=jnp.int32))
    return (summed * scale)[None]


def solution(mesh):
    placed = (
        P(None, "facet", None, None, "col"),
        P("facet"),
        P(),
        P(),
        P("col", None),
        P("col", None),
    )
    return jax.shard_map(
        per_device,
        mesh=mesh,
        in_specs=placed,
        out_specs=P("col", "facet", None, None),
        check_vma=False,
    )
```

profile of v0, /device:TPU:0, one launch (start us, length us, event | category | flops | bytes accessed | tf_op | source)
XLA Modules:
  0.0 140.9 jit_solution(5407549524900106008)
XLA Ops:
  6.5 0.0 reduce-scatter.2.cloned.1.call-start
  7.2 0.0 copy-start.3
  7.2 0.0 copy-start
  7.2 9.3 %fusion.16 = (f32[1024,512]{1,0:T(8,128)S(1)}, f32[1024,512]{1,0:T(8,128)S(1)}) fusion(s32[1024]{0:T(1024)S(1)} %get-tuple-element.42, s32[1024]{0:T(1024)S(1)} %get-tuple-element.43), kind=kLoop, calls=%fused_computation.29 | loop fusion | flops 14680064 | bytes 4202496 | tf_op jit(solution)/shard_map/cos | solution.py:68
  16.5 0.0 copy-done.3
  16.5 0.2 fusion.40
  16.8 0.0 copy-done
  16.8 0.3 fusion.62
  17.2 0.4 multiply_add_fusion
  17.6 0.4 pad_maximum_fusion
  18.0 10.6 %fusion = f32[768,1024]{1,0:T(8,128)S(1)} fusion(f32[768,1024]{1,0:T(8,128)S(1)} %bitcast.23, f32[1024,512]{1,0:T(8,128)S(1)} %get-tuple-element.39, f32[1024,512]{1,0:T(8,128)S(1)} %get-tuple-element.38), kind=kOutput, calls=%fused_computation | convolution fusion | flops 9664724992 | bytes 10485760 | tf_op jit(solution)/shard_map/dot_general | solution.py:28
  28.6 0.4 fusion.61
  29.0 0.3 slice_add_fusion.1
  29.3 0.0 copy-start.4
  29.4 0.0 copy-start.5
  29.4 0.0 copy-start.2
  29.4 1.3 pad_maximum_fusion.1
  30.7 0.0 reduce-scatter.2.cloned.1.call-update
  30.7 0.3 all-reduce.2.cloned.1.call-start
  31.0 0.0 copy-done.4
  31.0 0.0 copy-done.5
  31.0 0.6 constant_dynamic-slice_fusion
  33.5 0.6 fusion.63
  34.1 34.9 %reduce-scatter.2.cloned.1.call-done = f32[2,48,1024]{2,1,0:T(8,128)} async-done(((f32[8,48,1024]{2,1,0:T(8,128)}), f32[2,48,1024]{2,1,0:T(8,128)}) %reduce-scatter.2.cloned.1.call-update) | async-done | bytes 393232 | tf_op jit(solution)/shard_map/reduce_scatter | solution.py:69
  69.0 0.0 all-reduce.2.cloned.1.call-update
  69.0 1.2 and_select_fusion
  70.2 0.6 add_select_fusion.9
  70.9 54.4 %all-reduce.2.cloned.1.call-done = f32[2,48,1024]{2,1,0:T(8,128)} async-done(((f32[2,48,1024]{2,1,0:T(8,128)}), f32[2,48,1024]{2,1,0:T(8,128)}) %all-reduce.2.cloned.1.call-update) | async-done | bytes 393232 | tf_op jit(solution)/shard_map/psum | solution.py:84
  125.3 3.8 %fusion.25 = f32[512,1024]{1,0:T(8,128)S(1)} fusion(f32[2,48,1024]{2,1,0:T(8,128)} %all-reduce.2.cloned.1.call-done, s32[]{:T(128)S(6)} %select_n.215, s32[48]{0:T(128)S(1)} %get-tuple-element.44, s32[48]{0:T(128)S(1)} %get-tuple-element.45, s32[512]{0:T(512)S(1)} %add_select_fusion.9), kind=kOutput, calls=%fused_computation.48 | convolution fusion | flops 302678016 | bytes 2296196 | tf_op jit(solution)/shard_map/while/body/eval_jaxpr/dot_general | solution.py:46
  129.2 2.8 %fusion.23 = f32[512,1024]{1,0:T(8,128)S(1)} fusion(f32[2,48,1024]{2,1,0:T(8,128)S(1)} %copy-done.1, s32[]{:T(128)S(6)} %select_n.215, s32[48]{0:T(128)S(1)} %get-tuple-element.44, s32[48]{0:T(128)S(1)} %get-tuple-element.45, s32[512]{0:T(512)S(1)} %add_select_fusion.9), kind=kOutput, calls=%fused_computation.46 | convolution fusion | flops 302678016 | bytes 2296836 | tf_op jit(solution)/shard_map/while/body/eval_jaxpr/dot_general | solution.py:49
  132.0 0.5 fusion.14
  132.5 1.5 %maximum_multiply_fusion = f32[1,1,512,1024]{3,2,1,0:T(8,128)} fusion(f32[1,1,512,512]{3,2,1,0:T(8,128)S(1)} %get-tuple-element.18, f32[1,1,512,512]{3,2,1,0:T(8,128)S(1)} %get-tuple-element.17), kind=kLoop, calls=%fused_computation.17 | loop fusion | flops 1048576 | bytes 4194304 | tf_op jit(solution)/shard_map/mul | solution.py:91
  (6 shorter events, 0.1 us)
Async XLA Ops:
  6.5 62.5 %reduce-scatter.2.cloned.1.call-start = ((), (), s32[]{:S(2)}) async-start(), calls=%async_computation.1 | async-start | bytes 1966080 | tf_op jit(solution)/shard_map/reduce_scatter | solution.py:69
  7.2 9.3 %copy-start.3 = (s32[8]{0:T(128)S(1)}, s32[8]{0:T(128)}, u32[]{:S(2)}) copy-start(s32[8]{0:T(128)} %param.9) | copy-start | bytes 100
  7.2 9.6 %copy-start = (f32[2,1,24,2,1024]{4,3,2,1,0:T(2,128)S(1)}, f32[2,1,24,2,1024]{4,3,2,1,0:T(2,128)}, u32[]{:S(2)}) copy-start(f32[2,1,24,2,1024]{4,3,2,1,0:T(2,128)} %param.6) | copy-start | bytes 1179652
  29.3 1.6 %copy-start.4 = (s32[1,8]{1,0:T(1,128)S(1)}, s32[1,8]{1,0:T(1,128)}, u32[]{:S(2)}) copy-start(s32[1,8]{1,0:T(1,128)} %param.10) | copy-start | bytes 100
  29.4 1.6 %copy-start.5 = (s32[1,8]{1,0:T(1,128)S(1)}, s32[1,8]{1,0:T(1,128)}, u32[]{:S(2)}) copy-start(s32[1,8]{1,0:T(1,128)} %param.11) | copy-start | bytes 100
  29.4 4.1 %copy-start.2 = (s32[2]{0:T(128)S(1)}, s32[2]{0:T(128)}, u32[]{:S(2)}) copy-start(s32[2]{0:T(128)} %param.8) | copy-start | bytes 28
  30.7 94.6 %all-reduce.2.cloned.1.call-start = ((), (), s32[]{:S(2)}) async-start(), calls=%async_computation.2 | async-start | bytes 786432 | tf_op jit(solution)/shard_map/psum | solution.py:84
  125.3 3.8 %copy-start.1 = (f32[2,48,1024]{2,1,0:T(8,128)S(1)}, f32[2,48,1024]{2,1,0:T(8,128)}, u32[]{:S(2)}) copy-start(f32[2,48,1024]{2,1,0:T(8,128)} %all-reduce.2.cloned.1.call-done) | copy-start | bytes 1179652
Sparse Core Ops, SparseCore 0:
  30.8 38.1 reduce-scatter.1
  72.1 53.2 all-reduce.1
where the time goes:
time: 141 us
  waiting for transfers between devices  89.4 us (63%)
  matrix products  17.2 us (12%)
  between operations  16.2 us (11%)
  other arithmetic  15.9 us (11%)
  local copies, waits for them, and re-layouts  1.98 us (1%)
    psum x1, waiting for transfers between devices, per_device(): merged = lax.psum(owned, 'facet')  54.4 us
    reduce_scatter x1, waiting for transfers between devices, per_device(): lax.psum_scatter(column_part(real_part, imag_part, shifted, table, col_u,...  34.9 us
    dot_general x1, matrix products, column_part(): jnp.dot(stacked, table, precision=lax.Precision.HIGHEST, preferred_elemen...  10.6 us
    cos x1, other arithmetic, per_device(): jnp.cos(table_angle)  9.29 us
    dot_general x1, matrix products, slot_term(): jnp.dot(cosine, chosen, precision=lax.Precision.HIGHEST, preferred_elemen...  3.81 us
    dot_general x1, matrix products, slot_term(): jnp.dot(sine, chosen, precision=lax.Precision.HIGHEST, preferred_element_...  2.82 us
  transfers between devices with their start and end apart: 2, of which 2 were waited for; matrix products, arithmetic and copies ran while one was open for 2% of the time, Pallas kernels for 0%

commit v1 on v0

--- a/solution.py
+++ b/solution.py
@@ -81,7 +81,7 @@
     scale = 1.0 / math.sqrt(2.0 * FS * band_rows * lax.axis_size("facet"))
     owner_cols = slot_col[0]
     owner_shift = slot_v[0]
-    merged = lax.psum(owned, "facet")
+    merged = jnp.sum(lax.all_gather(owned, axis_name="facet"), axis=0)
 
     def own_slot(slot_id):
         return slot_term(merged, row_cells, img, owner_cols[slot_id], owner_shift[slot_id])

time: 141 us -> 119 us (0.84)
  waiting for transfers between devices: 89.4 us -> 65.8 us
  other arithmetic: 15.9 us -> 18.1 us
    psum x1 -> x0, waiting for transfers between devices: 54.4 us -> none  [per_device(): merged = lax.psum(owned, 'facet')]
    all_gather x0 -> x1, waiting for transfers between devices: none -> 27.7 us  [per_device(): merged = jnp.sum(lax.all_gather(owned, axis_name='facet'), axis=0)]
    reduce_scatter x1, waiting for transfers between devices: 34.9 us -> 38 us  [per_device(): lax.psum_scatter(column_part(real_part, imag_part, shifted, table, col_u,...]
    reduce_sum x0 -> x1, other arithmetic: none -> 2.17 us  [per_device(): merged = jnp.sum(lax.all_gather(owned, axis_name='facet'), axis=0)]
  transfers between devices with their start and end apart: 2 -> 2, of which waited for: 2 -> 2; matrix products, arithmetic and copies ran while one was open for 2% -> 3% of each run, Pallas kernels for 0% -> 0%
where the time goes in v1:
time: 119 us
  waiting for transfers between devices  65.8 us (55%)
  other arithmetic  18.1 us (15%)
  matrix products  16.2 us (14%)
  between operations  16.2 us (14%)
  local copies, waits for them, and re-layouts  2.04 us (2%)
    reduce_scatter x1, waiting for transfers between devices, per_device(): lax.psum_scatter(column_part(real_part, imag_part, shifted, table, col_u,...  38 us
    all_gather x1, waiting for transfers between devices, per_device(): merged = jnp.sum(lax.all_gather(owned, axis_name='facet'), axis=0)  27.7 us
    dot_general x1, matrix products, column_part(): jnp.dot(stacked, table, precision=lax.Precision.HIGHEST, preferred_elemen...  10.6 us
    cos x1, other arithmetic, per_device(): jnp.cos(table_angle)  9.29 us
    dot_general x1, matrix products, slot_term(): jnp.dot(sine, chosen, precision=lax.Precision.HIGHEST, preferred_element_...  2.82 us
    dot_general x1, matrix products, slot_term(): jnp.dot(cosine, chosen, precision=lax.Precision.HIGHEST, preferred_elemen...  2.82 us
  transfers between devices with their start and end apart: 2, of which 2 were waited for; matrix products, arithmetic and copies ran while one was open for 3% of the time, Pallas kernels for 0%

profile of v1, /device:TPU:0, one launch (start us, length us, event | category | flops | bytes accessed | tf_op | source)
XLA Modules:
  0.0 118.6 jit_solution(2886062862298222277)
XLA Ops:
  6.5 0.0 reduce-scatter.2.cloned.1.call-start
  7.2 0.0 copy-start.2
  7.2 0.0 copy-start
  7.2 9.3 %fusion.16 = (f32[1024,512]{1,0:T(8,128)S(1)}, f32[1024,512]{1,0:T(8,128)S(1)}) fusion(s32[1024]{0:T(1024)S(1)} %get-tuple-element.42, s32[1024]{0:T(1024)S(1)} %get-tuple-element.43), kind=kLoop, calls=%fused_computation.29 | loop fusion | flops 14680064 | bytes 4202496 | tf_op jit(solution)/shard_map/cos | solution.py:68
  16.5 0.0 copy-done.2
  16.5 0.2 fusion.40
  16.8 0.0 copy-done
  16.8 0.3 fusion.62
  17.2 0.4 multiply_add_fusion
  17.6 0.4 pad_maximum_fusion
  18.0 10.6 %fusion = f32[768,1024]{1,0:T(8,128)S(1)} fusion(f32[768,1024]{1,0:T(8,128)S(1)} %bitcast.24, f32[1024,512]{1,0:T(8,128)S(1)} %get-tuple-element.39, f32[1024,512]{1,0:T(8,128)S(1)} %get-tuple-element.38), kind=kOutput, calls=%fused_computation | convolution fusion | flops 9664724992 | bytes 10485760 | tf_op jit(solution)/shard_map/dot_general | solution.py:28
  28.6 0.4 fusion.61
  29.0 0.3 slice_add_fusion.1
  29.3 0.0 copy-start.3
  29.4 0.0 copy-start.4
  29.4 0.0 copy-start.1
  29.4 1.3 %pad_maximum_fusion.1 = f32[8,48,1024]{2,1,0:T(8,128)} fusion(f32[8,48,512]{2,1,0:T(8,128)S(1)} %get-tuple-element.20, f32[8,48,512]{2,1,0:T(8,128)S(1)} %get-tuple-element.19), kind=kLoop, calls=%fused_computation.21 | loop fusion | flops 393216 | bytes 3145728 | tf_op jit(solution)/shard_map/concatenate | solution.py:36
  30.7 0.0 reduce-scatter.2.cloned.1.call-update
  30.7 0.3 all-gather.3.cloned.1.call-start
  31.0 38.0 %reduce-scatter.2.cloned.1.call-done = f32[2,48,1024]{2,1,0:T(8,128)} async-done(((f32[8,48,1024]{2,1,0:T(8,128)}), f32[2,48,1024]{2,1,0:T(8,128)}) %reduce-scatter.2.cloned.1.call-update) | async-done | bytes 393232 | tf_op jit(solution)/shard_map/reduce_scatter | solution.py:69
  69.0 0.0 all-gather.3.cloned.1.call-update
  69.0 0.0 copy-done.3
  69.0 0.6 constant_dynamic-slice_fusion
  71.6 0.7 fusion.63
  72.3 1.4 %and_select_fusion = (s32[48]{0:T(128)S(1)}, s32[48]{0:T(128)S(1)}) fusion(s32[]{:T(128)} %bitcast.2, s32[]{:T(128)} %bitcast.1), kind=kLoop, calls=%fused_computation.91 | loop fusion | flops 2160 | bytes 392 | tf_op jit(solution)/shard_map/while/body/eval_jaxpr/jit(remainder)/select_n | solution.py:15
  73.6 0.6 add_select_fusion.9
  74.2 27.7 %all-gather.3.cloned.1.call-done = f32[16,48,1024]{2,1,0:T(8,128)} async-done(((f32[2,48,1024]{2,1,0:T(8,128)}), f32[16,48,1024]{2,1,0:T(8,128)}) %all-gather.3.cloned.1.call-update) | async-done | bytes 3145744 | tf_op jit(solution)/shard_map/all_gather | solution.py:84
  101.9 2.2 %reduce_sum.9 = f32[2,48,1024]{2,1,0:T(8,128)S(1)} reduce(f32[8,2,48,1024]{3,2,1,0:T(8,128)} %bitcast.25, f32[]{:T(128)} %constant.192.clone.1), dimensions={0}, to_apply=%region_1.2 | reduce | flops 688128 | bytes 3538948 | tf_op jit(solution)/shard_map/reduce_sum | solution.py:84
  104.1 2.8 %fusion.25 = f32[512,1024]{1,0:T(8,128)S(1)} fusion(f32[2,48,1024]{2,1,0:T(8,128)S(1)} %reduce_sum.9, s32[]{:T(128)S(6)} %select_n.215, s32[48]{0:T(128)S(1)} %get-tuple-element.44, s32[48]{0:T(128)S(1)} %get-tuple-element.45, s32[512]{0:T(512)S(1)} %add_select_fusion.9), kind=kOutput, calls=%fused_computation.48 | convolution fusion | flops 302678016 | bytes 2296836 | tf_op jit(solution)/shard_map/while/body/eval_jaxpr/dot_general | solution.py:46
  106.9 2.8 %fusion.23 = f32[512,1024]{1,0:T(8,128)S(1)} fusion(f32[2,48,1024]{2,1,0:T(8,128)S(1)} %reduce_sum.9, s32[]{:T(128)S(6)} %select_n.215, s32[48]{0:T(128)S(1)} %get-tuple-element.44, s32[48]{0:T(128)S(1)} %get-tuple-element.45, s32[512]{0:T(512)S(1)} %add_select_fusion.9), kind=kOutput, calls=%fused_computation.46 | convolution fusion | flops 302678016 | bytes 2296836 | tf_op jit(solution)/shard_map/while/body/eval_jaxpr/dot_general | solution.py:49
  109.8 0.5 fusion.14
  110.3 1.5 %maximum_multiply_fusion = f32[1,1,512,1024]{3,2,1,0:T(8,128)} fusion(f32[1,1,512,512]{3,2,1,0:T(8,128)S(1)} %get-tuple-element.18, f32[1,1,512,512]{3,2,1,0:T(8,128)S(1)} %get-tuple-element.17), kind=kLoop, calls=%fused_computation.17 | loop fusion | flops 1048576 | bytes 4194304 | tf_op jit(solution)/shard_map/mul | solution.py:91
  (5 shorter events, 0.1 us)
Async XLA Ops:
  6.5 62.5 %reduce-scatter.2.cloned.1.call-start = ((), (), s32[]{:S(2)}) async-start(), calls=%async_computation.1 | async-start | bytes 1966080 | tf_op jit(solution)/shard_map/reduce_scatter | solution.py:69
  7.2 9.3 %copy-start.2 = (s32[8]{0:T(128)S(1)}, s32[8]{0:T(128)}, u32[]{:S(2)}) copy-start(s32[8]{0:T(128)} %param.9) | copy-start | bytes 100
  7.2 9.6 %copy-start = (f32[2,1,24,2,1024]{4,3,2,1,0:T(2,128)S(1)}, f32[2,1,24,2,1024]{4,3,2,1,0:T(2,128)}, u32[]{:S(2)}) copy-start(f32[2,1,24,2,1024]{4,3,2,1,0:T(2,128)} %param.6) | copy-start | bytes 1179652
  29.3 39.7 %copy-start.3 = (s32[1,8]{1,0:T(1,128)S(1)}, s32[1,8]{1,0:T(1,128)}, u32[]{:S(2)}) copy-start(s32[1,8]{1,0:T(1,128)} %param.10) | copy-start | bytes 100
  29.4 39.7 %copy-start.4 = (s32[1,8]{1,0:T(1,128)S(1)}, s32[1,8]{1,0:T(1,128)}, u32[]{:S(2)}) copy-start(s32[1,8]{1,0:T(1,128)} %param.11) | copy-start | bytes 100
  29.4 42.2 %copy-start.1 = (s32[2]{0:T(128)S(1)}, s32[2]{0:T(128)}, u32[]{:S(2)}) copy-start(s32[2]{0:T(128)} %param.8) | copy-start | bytes 28
  30.7 71.3 %all-gather.3.cloned.1.call-start = ((), (), s32[]{:S(2)}) async-start(), calls=%async_computation.2 | async-start | bytes 3538944 | tf_op jit(solution)/shard_map/all_gather | solution.py:84
Sparse Core Ops, SparseCore 0:
  30.8 38.1 reduce-scatter.1
  70.9 31.0 all-gather.2
